TPU v7x, 32 devices: a whole 2x2x4 slice. The times are simulated.
32 devices in a mesh: groups: 2 (over y), aa: 4 (over z), ba: 4 (over x, core).
Axes of the slice: x: 2, y: 2, z: 4, core: 2. Of those that a mesh axis runs over, the one named last changes fastest.
Arguments:
- alignment_state: bfloat16 [64, 128, 256], P(('groups', 'aa'), 'ba'), parts along dimension 0, may hold values from -1.5 to 1.5
- pair_state: bfloat16 [256, 128, 128], P(('groups', 'aa'), 'ba'), parts along dimension 0, may hold values from -1.796875 to 1.796875
- alignment_mask: int32 [64, 128], P(('groups', 'aa'), 'ba'), parts along dimension 0, may hold values from 0 to 1, as said below
- left_weight: bfloat16 [256, 32], replicated, may hold values from -0.375 to 0.375
- right_weight: bfloat16 [256, 32], replicated, may hold values from -0.375 to 0.375
- outer_output_weight: bfloat16 [1024, 128], replicated, may hold values from -0.75 to 0.75
- pair_bias_weight: bfloat16 [128, 8], replicated, may hold values from -40 to 40
- query_weight: bfloat16 [256, 256], replicated, may hold values from -0.375 to 0.375
- key_weight: bfloat16 [256, 256], replicated, may hold values from -0.375 to 0.375
- value_weight: bfloat16 [256, 256], replicated, may hold values from -0.375 to 0.375
- gate_weight: bfloat16 [256, 256], replicated, may hold values from -0.375 to 0.375
- output_weight: bfloat16 [256, 256], replicated, may hold values from -1.5 to 1.5
- up_weight: bfloat16 [256, 1024], replicated, may hold values from -0.375 to 0.375
- down_weight: bfloat16 [1024, 256], replicated, may hold values from -0.1875 to 0.1875
Outputs:
- alignment_output: bfloat16 [64, 128, 256], P(('groups', 'aa'), 'ba'), parts along dimension 0
- pair_output: bfloat16 [256, 128, 128], P(('groups', 'aa'), 'ba'), parts along dimension 0
There are 2 independent parts, one for each index of `groups`. A program takes and returns all parts, laid end to end along the dimension named above; an argument that names none is the same for every part. Nothing has to cross between parts.
Inputs may be any that keep to these rules, and one draw needn't show every extreme that they name: `alignment_mask`: every residue of the first sequence is kept (mask 1); other entries are kept at random.
All inputs are finite; a program needn't handle non-finite values.
Results may differ from a plain program's by a relative error of at most 0.013.
The roundings to bfloat16 on the way count: a program that leaves them out, or rounds other values in their place, can miss the bound.
Values may be sent and summed in bfloat16 or wider, within the bound.
No kernel may reach another device: no remote copies, remote signals or barrier semaphores. Data moves between devices by JAX's collectives and lax.ppermute only.
A program may use at most 128 MiB of HBM per device.

v0:
```python
import jax
import jax.numpy as jnp
from jax import lax
from jax.sharding import PartitionSpec as P


def from_root(x, axis, root):
    mine = lax.axis_index(axis) == root
    return lax.psum(jnp.where(mine, x, jnp.zeros_like(x)), axis)


def row_norm_input(values):
    center = values - jnp.mean(values, axis=-1, keepdims=True)
    spread = jnp.mean(center * center, axis=-1, keepdims=True)
    return center * lax.rsqrt(spread + 1e-05)


def attend_block(carried, query_all, key_piece, value_piece, valid_piece, bias_part):
    top_old, mass_old, accum_old = carried
    scores = (
        jnp.einsum("sihd,sjhd->shij", query_all, key_piece, preferred_element_type=jnp.float32)
        + bias_part[None]
    )
    scores = jnp.where(valid_piece[:, None, None, :] > 0, scores, -1000000000.0)
    new_top = jnp.maximum(top_old, jnp.max(scores, axis=-1))
    weights_raw = jnp.exp(scores - new_top[:, :, :, None])
    mass_new = jnp.sum(weights_raw, axis=-1)
    accum_new = jnp.einsum(
        "shij,sjhd->shid",
        weights_raw.astype(jnp.bfloat16),
        value_piece,
        preferred_element_type=jnp.float32,
    )
    return (new_top, mass_new, accum_new)


def per_device(
    alignment_state,
    pair_state,
    alignment_mask,
    left_weight,
    right_weight,
    outer_output_weight,
    pair_bias_weight,
    query_weight,
    key_weight,
    value_weight,
    gate_weight,
    output_weight,
    up_weight,
    down_weight,
):
    sequence_count, residue_count, channel_count = alignment_state.shape
    opm_width = left_weight.shape[1]
    num_heads = pair_bias_weight.shape[1]
    head_width = query_weight.shape[1] // num_heads
    layer_normed = row_norm_input(alignment_state.astype(jnp.float32)).astype(jnp.bfloat16)
    flat_rows = layer_normed.reshape(sequence_count * residue_count, channel_count)
    row_keep_mask = alignment_mask.astype(jnp.float32)
    keep_half = row_keep_mask.astype(jnp.bfloat16)
    left_fac = (
        jnp.dot(flat_rows, left_weight, preferred_element_type=jnp.float32).reshape(
            sequence_count, residue_count, opm_width
        )
        * row_keep_mask[:, :, None]
    ).astype(jnp.bfloat16)
    right_fac = (
        jnp.dot(flat_rows, right_weight, preferred_element_type=jnp.float32).reshape(
            sequence_count, residue_count, opm_width
        )
        * row_keep_mask[:, :, None]
    ).astype(jnp.bfloat16)
    col_left, col_right, col_keep = (
        lax.all_gather(left_fac, "aa", axis=0, tiled=True),
        lax.all_gather(right_fac, "aa", axis=0, tiled=True),
        lax.all_gather(keep_half, "aa", axis=0, tiled=True),
    )
    row_left, row_keep = (
        from_root(col_left, "ba", lax.axis_index("aa")),
        from_root(col_keep, "ba", lax.axis_index("aa")),
    )
    seq_total = col_right.shape[0]
    pair_count = jnp.dot(row_keep.T, col_keep, preferred_element_type=jnp.float32)
    left_flat = row_left.reshape(seq_total, residue_count * opm_width)
    right_flat = col_right.reshape(seq_total, residue_count * opm_width)
    row_block = 8

    def outer_block(block_index):
        left_part = lax.dynamic_slice_in_dim(
            left_flat, block_index * (row_block * opm_width), row_block * opm_width, 1
        )
        outer_sum = lax.dot_general(
            left_part, right_flat, (((0,), (0,)), ((), ())), preferred_element_type=jnp.float32
        )
        outer_sum = outer_sum.reshape(row_block, opm_width, residue_count, opm_width).transpose(
            0, 2, 1, 3
        )
        outer_sum = outer_sum.reshape(row_block * residue_count, opm_width * opm_width).astype(
            jnp.bfloat16
        )
        return jnp.dot(outer_sum, outer_output_weight, preferred_element_type=jnp.float32).reshape(
            row_block, residue_count, -1
        )

    update = lax.map(outer_block, jnp.arange(residue_count // row_block, dtype=jnp.int32)).reshape(
        residue_count, residue_count, -1
    )
    pair_output = (pair_state.astype(jnp.float32) + update / pair_count[:, :, None]).astype(
        jnp.bfloat16
    )
    pair_normed = row_norm_input(pair_output.astype(jnp.float32)).astype(jnp.bfloat16)
    tile_bias = jnp.dot(
        pair_normed.reshape(residue_count * residue_count, -1),
        pair_bias_weight,
        preferred_element_type=jnp.float32,
    )
    tile_bias = tile_bias.reshape(residue_count, residue_count, num_heads).transpose(2, 0, 1)
    rows_bias = lax.all_gather(tile_bias, "ba", axis=2, tiled=True)
    bias_here = from_root(rows_bias, "aa", lax.axis_index("ba"))
    score_scale = head_width ** (-0.5)
    query_all = (
        (jnp.dot(flat_rows, query_weight, preferred_element_type=jnp.float32) * score_scale)
        .astype(jnp.bfloat16)
        .reshape(sequence_count, residue_count, num_heads, head_width)
    )
    gate_act = jax.nn.sigmoid(jnp.dot(flat_rows, gate_weight, preferred_element_type=jnp.float32))
    start_state = (
        jnp.full((sequence_count, num_heads, residue_count), -1e30, jnp.float32),
        jnp.zeros((sequence_count, num_heads, residue_count), jnp.float32),
        jnp.zeros((sequence_count, num_heads, residue_count, head_width), jnp.float32),
    )
    w_pair = jnp.concatenate((key_weight, value_weight), axis=1)
    rows_in = lax.all_gather(layer_normed, "ba", axis=1, tiled=True)
    valid_piece = lax.all_gather(keep_half, "ba", axis=1, tiled=True)
    span_len = rows_in.shape[1]
    key_value = jnp.dot(
        rows_in.reshape(sequence_count * span_len, channel_count),
        w_pair,
        preferred_element_type=jnp.float32,
    ).astype(jnp.bfloat16)
    key_value = key_value.reshape(sequence_count, span_len, 2, num_heads, head_width)
    final_state = attend_block(
        start_state, query_all, key_value[:, :, 0], key_value[:, :, 1], valid_piece, bias_here
    )
    attended = final_state[2] / final_state[1][:, :, :, None]
    attended = attended.transpose(0, 2, 1, 3).reshape(
        sequence_count * residue_count, num_heads * head_width
    )
    gated_row_output = (attended * gate_act).astype(jnp.bfloat16)
    alignment_middle = alignment_state.astype(jnp.float32) + jnp.dot(
        gated_row_output, output_weight, preferred_element_type=jnp.float32
    ).reshape(sequence_count, residue_count, channel_count)
    middle_normed = (
        row_norm_input(alignment_middle)
        .astype(jnp.bfloat16)
        .reshape(sequence_count * residue_count, channel_count)
    )
    hidden_units = jax.nn.relu(
        jnp.dot(middle_normed, up_weight, preferred_element_type=jnp.float32)
    ).astype(jnp.bfloat16)
    alignment_output = (
        alignment_middle
        + jnp.dot(hidden_units, down_weight, preferred_element_type=jnp.float32).reshape(
            sequence_count, residue_count, channel_count
        )
    ).astype(jnp.bfloat16)
    return (alignment_output, pair_output)


def solution(mesh):
    return jax.shard_map(
        per_device,
        mesh=mesh,
        in_specs=(
            P(("groups", "aa"), "ba", None),
            P(("groups", "aa"), "ba", None),
            P(("groups", "aa"), "ba"),
            P(),
            P(),
            P(),
            P(),
            P(),
            P(),
            P(),
            P(),
            P(),
            P(),
            P(),
        ),
        out_specs=(P(("groups", "aa"), "ba", None), P(("groups", "aa"), "ba", None)),
        check_vma=False,
    )
```

profile of v0, /device:TPU:0, one launch (start us, length us, event | category | flops | bytes accessed | tf_op | source)
XLA Modules:
  0.0 188.1 jit_solution(4134955716603868108)
XLA Ops:
  12.1 15.7 %all_gather.20 = bf16[32,32,32]{2,1,0:T(8,128)(2,1)S(1)} all-gather(bf16[8,32,32]{2,1,0:T(8,128)(2,1)S(1)} %fusion.15), channel_id=1, replica_groups=mesh['groups'=2,'aa'=4,'ba'=4] {'aa'}, dimensions={0}, use_global_device_ids=true | all-gather | bytes 81920 | tf_op jit(solution)/shard_map/all_gather | solution.py:74
  28.8 7.2 %all_gather.19 = bf16[8,128,256]{2,1,0:T(8,128)(2,1)S(1)} all-gather(bf16[8,32,256]{2,1,0:T(8,128)(2,1)S(1)} %fusion.31), channel_id=1, replica_groups=mesh['groups'=2,'aa'=4,'ba'=4] {'ba'}, dimensions={1}, use_global_device_ids=true | all-gather | bytes 655360 | tf_op jit(solution)/shard_map/all_gather | solution.py:133
  36.1 12.0 %all_gather.22 = bf16[32,32]{1,0:T(8,128)(2,1)S(1)} all-gather(bf16[8,32]{1,0:T(8,128)(2,1)S(1)} %get-tuple-element.49), channel_id=1, replica_groups=mesh['groups'=2,'aa'=4,'ba'=4] {'aa'}, dimensions={0}, use_global_device_ids=true | all-gather | bytes 2560 | tf_op jit(solution)/shard_map/all_gather | solution.py:76
  48.1 5.8 %psum.22 = bf16[32,32]{1,0:T(8,128)(2,1)S(1)} all-reduce(bf16[32,32]{1,0:T(8,128)(2,1)S(1)} %broadcast_select_fusion.2), channel_id=1, replica_groups=mesh['groups'=2,'aa'=4,'ba'=4] {'ba'}, use_global_device_ids=true, to_apply=%region_5.6 | all-reduce | flops 1024 | bytes 4096 | tf_op jit(solution)/shard_map/psum | solution.py:9
  56.6 13.9 %all_gather.21 = bf16[32,32,32]{2,1,0:T(8,128)(2,1)S(1)} all-gather(bf16[8,32,32]{2,1,0:T(8,128)(2,1)S(1)} %fusion.16), channel_id=1, replica_groups=mesh['groups'=2,'aa'=4,'ba'=4] {'aa'}, dimensions={0}, use_global_device_ids=true | all-gather | bytes 81920 | tf_op jit(solution)/shard_map/all_gather | solution.py:75
  72.4 5.6 %all-gather = bf16[4,32,8]{1,2,0:T(8,128)(2,1)} all-gather(bf16[1,32,8]{1,2,0:T(8,128)(2,1)S(1)} %bitcast.97), channel_id=1, replica_groups=mesh['groups'=2,'aa'=4,'ba'=4] {'ba'}, dimensions={0}, use_global_device_ids=true | all-gather | bytes 2560 | tf_op jit(solution)/shard_map/all_gather | solution.py:134
  78.6 45.7 %while.10 = (s32[]{:T(128)}, f32[4,8,32,128]{3,2,1,0:T(8,128)}, s32[4]{0:T(128)}, bf16[32,1024]{1,0:T(8,128)(2,1)}, bf16[32,1024]{1,0:T(8,128)(2,1)}, /*index=5*...) while((s32[]{:T(128)}, f32[4,8,32,128]{3,2,1,0:T(8,128)}, s32[4]{0:T(128)}, ...), condition=%wide.region_4.5_spmd, body=%wide.region_3.4_spmd.sunk | while | flops 84148224 | bytes 4670115 | solution.py:105
  78.6 1.3 dynamic_slice.12
  80.6 1.2 convolution_convert_fusion.3
  81.8 1.6 convert_element_type.141
  83.4 2.2 %copy.52 = bf16[8,32,32,32]{3,2,1,0:T(8,128)(2,1)} copy(bf16[8,32,32,32]{3,1,2,0:T(8,128)(2,1)S(1)} %bitcast.86) | data formatting | bytes 1048576 | tf_op jit(solution)/shard_map/while/body/eval_jaxpr/convert_element_type | solution.py:98
  85.5 3.5 %convert_element_type.142 = bf16[8,32,1024]{2,1,0:T(8,128)(2,1)S(1)} reshape(bf16[8,32,32,32]{3,2,1,0:T(8,128)(2,1)} %copy.52) | data formatting | bytes 1048576 | tf_op jit(solution)/shard_map/while/body/eval_jaxpr/convert_element_type | solution.py:98
  90.0 1.3 dynamic_slice.12
  92.0 1.2 convolution_convert_fusion.3
  93.2 1.6 convert_element_type.141
  94.8 2.2 %copy.52 = bf16[8,32,32,32]{3,2,1,0:T(8,128)(2,1)} copy(bf16[8,32,32,32]{3,1,2,0:T(8,128)(2,1)S(1)} %bitcast.86) | data formatting | bytes 1048576 | tf_op jit(solution)/shard_map/while/body/eval_jaxpr/convert_element_type | solution.py:98
  96.9 3.5 %convert_element_type.142 = bf16[8,32,1024]{2,1,0:T(8,128)(2,1)S(1)} reshape(bf16[8,32,32,32]{3,2,1,0:T(8,128)(2,1)} %copy.52) | data formatting | bytes 1048576 | tf_op jit(solution)/shard_map/while/body/eval_jaxpr/convert_element_type | solution.py:98
  101.4 1.3 dynamic_slice.12
  103.4 1.2 convolution_convert_fusion.3
  104.6 1.6 convert_element_type.141
  106.2 2.2 %copy.52 = bf16[8,32,32,32]{3,2,1,0:T(8,128)(2,1)} copy(bf16[8,32,32,32]{3,1,2,0:T(8,128)(2,1)S(1)} %bitcast.86) | data formatting | bytes 1048576 | tf_op jit(solution)/shard_map/while/body/eval_jaxpr/convert_element_type | solution.py:98
  108.4 3.5 %convert_element_type.142 = bf16[8,32,1024]{2,1,0:T(8,128)(2,1)S(1)} reshape(bf16[8,32,32,32]{3,2,1,0:T(8,128)(2,1)} %copy.52) | data formatting | bytes 1048576 | tf_op jit(solution)/shard_map/while/body/eval_jaxpr/convert_element_type | solution.py:98
  112.8 1.3 dynamic_slice.12
  114.8 1.2 convolution_convert_fusion.3
  116.0 1.6 convert_element_type.141
  117.6 2.2 %copy.52 = bf16[8,32,32,32]{3,2,1,0:T(8,128)(2,1)} copy(bf16[8,32,32,32]{3,1,2,0:T(8,128)(2,1)S(1)} %bitcast.86) | data formatting | bytes 1048576 | tf_op jit(solution)/shard_map/while/body/eval_jaxpr/convert_element_type | solution.py:98
  119.8 3.5 %convert_element_type.142 = bf16[8,32,1024]{2,1,0:T(8,128)(2,1)S(1)} reshape(bf16[8,32,32,32]{3,2,1,0:T(8,128)(2,1)} %copy.52) | data formatting | bytes 1048576 | tf_op jit(solution)/shard_map/while/body/eval_jaxpr/convert_element_type | solution.py:98
  124.3 1.3 fusion.24
  126.3 1.2 convolution_bitcast_fusion.2
  127.6 7.3 %all_gather.23 = f32[8,32,128]{1,0,2:T(8,128)S(1)} all-gather(f32[8,32,32]{1,0,2:T(8,128)S(1)} %copy.34), channel_id=1, replica_groups=mesh['groups'=2,'aa'=4,'ba'=4] {'ba'}, dimensions={2}, use_global_device_ids=true | all-gather | bytes 163840 | tf_op jit(solution)/shard_map/all_gather | solution.py:118
  135.9 38.8 %all-reduce.5.cloned.1.call-done = f32[8,32,128]{1,0,2:T(8,128)} async-done(((f32[8,32,128]{1,0,2:T(8,128)}), f32[8,32,128]{1,0,2:T(8,128)}) %all-reduce.5.cloned.1.call-update) | async-done | bytes 131088 | tf_op jit(solution)/shard_map/psum | solution.py:9
  174.6 1.2 copy.35
  (83 shorter events, 21.8 us)
Async XLA Ops:
  7.2 172.8 %copy-start = (bf16[1024,256]{1,0:T(8,128)(2,1)S(1)}, bf16[1024,256]{1,0:T(8,128)(2,1)}, u32[]{:S(2)}) copy-start(bf16[1024,256]{1,0:T(8,128)(2,1)} %param.29) | copy-start | bytes 1572868
  7.2 28.8 %copy-start.11 = (bf16[256,32]{0,1:T(8,128)(2,1)S(1)}, bf16[256,32]{0,1:T(8,128)(2,1)}, u32[]{:S(2)}) copy-start(bf16[256,32]{0,1:T(8,128)(2,1)} %param.20) | copy-start | bytes 49156
  7.2 46.7 %copy-start.8 = (bf16[256,256]{1,0:T(8,128)(2,1)S(1)}, bf16[256,256]{1,0:T(8,128)(2,1)}, u32[]{:S(2)}) copy-start(bf16[256,256]{1,0:T(8,128)(2,1)} %param.24) | copy-start | bytes 393220
  7.2 46.7 %copy-start.7 = (bf16[256,256]{1,0:T(8,128)(2,1)S(1)}, bf16[256,256]{1,0:T(8,128)(2,1)}, u32[]{:S(2)}) copy-start(bf16[256,256]{1,0:T(8,128)(2,1)} %param.25) | copy-start | bytes 393220
  7.2 70.8 %all-reduce.3.cloned.1.call-start = ((), (), s32[]{:S(2)}) async-start(), calls=%async_computation | async-start | bytes 131072 | tf_op jit(solution)/shard_map/psum | solution.py:9
  28.7 145.9 %all-reduce.5.cloned.1.call-start = ((), (), s32[]{:S(2)}) async-start(), calls=%async_computation.1 | async-start | bytes 1048576 | tf_op jit(solution)/shard_map/psum | solution.py:9
  54.9 1.4 copy-start.9
  55.2 23.4 %copy-start.1 = (bf16[1024,128]{1,0:T(8,128)(2,1)S(1)}, bf16[1024,128]{1,0:T(8,128)(2,1)}, u32[]{:S(2)}) copy-start(bf16[1024,128]{1,0:T(8,128)(2,1)} %param.21) | copy-start | bytes 786436
  125.6 50.3 %copy-start.3 = (bf16[32,32,128]{2,1,0:T(8,128)(2,1)}, bf16[32,32,128]{2,1,0:T(8,128)(2,1)S(1)}, u32[]{:S(2)}) copy-start(bf16[32,32,128]{2,1,0:T(8,128)(2,1)S(1)} %fusion.24) | copy-start | bytes 786436
  125.6 10.1 %copy-start.10 = (bf16[4,32,8]{1,2,0:T(8,128)(2,1)S(1)}, bf16[4,32,8]{1,2,0:T(8,128)(2,1)}, u32[]{:S(2)}) copy-start(bf16[4,32,8]{1,2,0:T(8,128)(2,1)} %all-gather) | copy-start | bytes 6148
  125.8 50.0 %copy-start.4 = (bf16[8,32,8,32]{3,2,1,0:T(8,128)(2,1)S(1)}, bf16[8,32,8,32]{3,2,1,0:T(8,128)(2,1)}, u32[]{:S(2)}) copy-start(bf16[8,32,8,32]{3,2,1,0:T(8,128)(2,1)} %reshape.109) | copy-start | bytes 393220
  125.8 50.0 %copy-start.6 = (bf16[8,128,1,8,32]{1,0,4,3,2:T(8,128)(2,1)S(1)}, bf16[8,128,1,8,32]{1,0,4,3,2:T(8,128)(2,1)}, u32[]{:S(2)}) copy-start(bf16[8,128,1,8,32]{1,0,4,3,2:T(8,128)(2,1)} %get-tuple-element.48) | copy-start | bytes 1572868
  135.9 41.2 %copy-start.5 = (bf16[8,128,1,8,32]{1,0,4,3,2:T(8,128)(2,1)S(1)}, bf16[8,128,1,8,32]{1,0,4,3,2:T(8,128)(2,1)}, u32[]{:S(2)}) copy-start(bf16[8,128,1,8,32]{1,0,4,3,2:T(8,128)(2,1)} %get-tuple-element.47) | copy-start | bytes 1572868
  178.2 1.0 copy-start.13
  178.2 1.0 copy-start.14
  178.2 1.3 copy-start.2
  178.8 1.2 copy-start.12
Sparse Core Ops, SparseCore 0:
  28.9 33.0 all-reduce.2
  135.9 38.7 all-reduce.4
where the time goes:
time: 189 us; the launch traced here: 188 us
  blocking collectives  67.4 us (36%)
  local copies, waits for them, and re-layouts  42 us (22%)
  waiting for transfers between devices  38.8 us (21%)
  between operations  14.5 us (8%)
  matrix products  14 us (7%)
  other arithmetic  8.53 us (5%)
  loops' own time  2.9 us (2%)
    psum x2, waiting for transfers between devices, from_root(): return lax.psum(jnp.where(mine, x, jnp.zeros_like(x)), axis)  38.8 us
    convert_element_type x12, local copies, waits for them, and re-layouts, outer_block(): outer_sum.reshape(row_block * residue_count, opm_width * opm_width)  29.1 us
    all_gather x1, blocking collectives, per_device(): lax.all_gather(left_fac, 'aa', axis=0, tiled=True)  15.7 us
    all_gather x1, blocking collectives, per_device(): lax.all_gather(right_fac, 'aa', axis=0, tiled=True)  13.9 us
    all_gather x1, blocking collectives, per_device(): lax.all_gather(keep_half, 'aa', axis=0, tiled=True)  12 us
    all_gather x1, blocking collectives, per_device(): rows_bias = lax.all_gather(tile_bias, 'ba', axis=2, tiled=True)  7.28 us
    all_gather x1, blocking collectives, per_device(): rows_in = lax.all_gather(layer_normed, 'ba', axis=1, tiled=True)  7.17 us
    psum x1, blocking collectives, from_root(): return lax.psum(jnp.where(mine, x, jnp.zeros_like(x)), axis)  5.76 us
  transfers between devices with their start and end apart: 2, of which 1 were waited for; matrix products, arithmetic and copies ran while one was open for 3% of the time, Pallas kernels for 0%

commit v1 on v0

--- a/solution.py
+++ b/solution.py
@@ -4,9 +4,15 @@
 from jax.sharding import PartitionSpec as P
 
 
+def add_all(x, axis):
+    parts = lax.all_gather(x, axis, axis=0, tiled=False)
+    total = parts.sum(axis=0)
+    return total
+
+
 def from_root(x, axis, root):
     mine = lax.axis_index(axis) == root
-    return lax.psum(jnp.where(mine, x, jnp.zeros_like(x)), axis)
+    return add_all(jnp.where(mine, x, jnp.zeros_like(x)), axis)
 
 
 def row_norm_input(values):

time: 189 us -> 178 us (0.942)
  blocking collectives: 67.4 us -> 115 us
  waiting for transfers between devices: 38.8 us -> 0 us
  between operations: 14.5 us -> 0.99 us
  local copies, waits for them, and re-layouts: 42 us -> 36.6 us
    all_gather x0 -> x3, blocking collectives: none -> 53.6 us  [add_all(): parts = lax.all_gather(x, axis, axis=0, tiled=False)]
    psum x2 -> x0, waiting for transfers between devices: 38.8 us -> none  [from_root(): return lax.psum(jnp.where(mine, x, jnp.zeros_like(x)), axis)]
    psum x1 -> x0, blocking collectives: 5.76 us -> none  [from_root(): return lax.psum(jnp.where(mine, x, jnp.zeros_like(x)), axis)]
    dynamic_slice x4, local copies, waits for them, and re-layouts: 5.27 us -> 2.65 us  [per_device(): lax.map(outer_block, jnp.arange(residue_count // row_block, dtype=jnp.int...]
  transfers between devices with their start and end apart: 2 -> 0, of which waited for: 1 -> 0; matrix products, arithmetic and copies ran while one was open for 3% -> 0% of each run, Pallas kernels for 0% -> 0%
where the time goes in v1:
time: 178 us; the launch traced here: 177 us
  blocking collectives  115 us (65%)
  local copies, waits for them, and re-layouts  36.6 us (21%)
  matrix products  13.3 us (7%)
  other arithmetic  8.38 us (5%)
  loops' own time  2.9 us (2%)
    all_gather x3, blocking collectives, add_all(): parts = lax.all_gather(x, axis, axis=0, tiled=False)  53.6 us
    convert_element_type x12, local copies, waits for them, and re-layouts, outer_block(): outer_sum.reshape(row_block * residue_count, opm_width * opm_width)  29.1 us
    all_gather x1, blocking collectives, per_device(): lax.all_gather(left_fac, 'aa', axis=0, tiled=True)  15.7 us
    all_gather x1, blocking collectives, per_device(): lax.all_gather(right_fac, 'aa', axis=0, tiled=True)  14.3 us
    all_gather x1, blocking collectives, per_device(): lax.all_gather(keep_half, 'aa', axis=0, tiled=True)  12.2 us
    all_gather x1, blocking collectives, per_device(): rows_bias = lax.all_gather(tile_bias, 'ba', axis=2, tiled=True)  7.28 us
    all_gather x1, blocking collectives, per_device(): rows_in = lax.all_gather(layer_normed, 'ba', axis=1, tiled=True)  6.51 us
    all_gather x1, blocking collectives, per_device(): valid_piece = lax.all_gather(keep_half, 'ba', axis=1, tiled=True)  5.37 us

profile of v1, /device:TPU:0, one launch (start us, length us, event | category | flops | bytes accessed | tf_op | source)
XLA Modules:
  0.0 177.2 jit_solution(13666760070082602428)
XLA Ops:
  0.6 1.1 convert_reduce_fusion.1
  1.7 1.1 fusion.30
  2.9 1.0 fusion.31
  5.5 15.7 %all_gather.38 = bf16[32,32,32]{2,1,0:T(8,128)(2,1)S(1)} all-gather(bf16[8,32,32]{2,1,0:T(8,128)(2,1)S(1)} %fusion.15), channel_id=1, replica_groups=mesh['groups'=2,'aa'=4,'ba'=4] {'aa'}, dimensions={0}, use_global_device_ids=true | all-gather | bytes 81920 | tf_op jit(solution)/shard_map/all_gather | solution.py:80
  21.2 10.2 %all-gather = bf16[128,32,32]{2,1,0:T(8,128)(2,1)S(1)} all-gather(bf16[32,32,32]{2,1,0:T(8,128)(2,1)S(1)} %broadcast_select_fusion.1), channel_id=2, replica_groups=mesh['groups'=2,'aa'=4,'ba'=4] {'ba'}, dimensions={0}, use_global_device_ids=true | all-gather | bytes 327680 | tf_op jit(solution)/shard_map/all_gather | solution.py:8
  32.7 14.3 %all_gather.41 = bf16[32,32,32]{2,1,0:T(8,128)(2,1)S(1)} all-gather(bf16[8,32,32]{2,1,0:T(8,128)(2,1)S(1)} %fusion.16), channel_id=1, replica_groups=mesh['groups'=2,'aa'=4,'ba'=4] {'aa'}, dimensions={0}, use_global_device_ids=true | all-gather | bytes 81920 | tf_op jit(solution)/shard_map/all_gather | solution.py:81
  47.9 43.1 %while.10 = (s32[]{:T(128)}, f32[4,8,32,128]{3,2,1,0:T(8,128)}, s32[4]{0:T(128)S(1)}, bf16[32,1024]{1,0:T(8,128)(2,1)}, bf16[32,1024]{1,0:T(8,128)(2,1)}, /*inde...) while((s32[]{:T(128)}, f32[4,8,32,128]{3,2,1,0:T(8,128)}, ...), condition=%wide.region_4.5_spmd, body=%wide.region_3.4_spmd.sunk | while | flops 84148224 | bytes 4670115 | solution.py:111
  49.3 1.2 convolution_convert_fusion.3
  50.5 1.6 convert_element_type.145
  52.1 2.2 %copy.53 = bf16[8,32,32,32]{3,2,1,0:T(8,128)(2,1)} copy(bf16[8,32,32,32]{3,1,2,0:T(8,128)(2,1)S(1)} %bitcast.90) | data formatting | bytes 1048576 | tf_op jit(solution)/shard_map/while/body/eval_jaxpr/convert_element_type | solution.py:104
  54.3 3.5 %convert_element_type.146 = bf16[8,32,1024]{2,1,0:T(8,128)(2,1)S(1)} reshape(bf16[8,32,32,32]{3,2,1,0:T(8,128)(2,1)} %copy.53) | data formatting | bytes 1048576 | tf_op jit(solution)/shard_map/while/body/eval_jaxpr/convert_element_type | solution.py:104
  60.1 1.2 convolution_convert_fusion.3
  61.3 1.6 convert_element_type.145
  62.9 2.2 %copy.53 = bf16[8,32,32,32]{3,2,1,0:T(8,128)(2,1)} copy(bf16[8,32,32,32]{3,1,2,0:T(8,128)(2,1)S(1)} %bitcast.90) | data formatting | bytes 1048576 | tf_op jit(solution)/shard_map/while/body/eval_jaxpr/convert_element_type | solution.py:104
  65.0 3.5 %convert_element_type.146 = bf16[8,32,1024]{2,1,0:T(8,128)(2,1)S(1)} reshape(bf16[8,32,32,32]{3,2,1,0:T(8,128)(2,1)} %copy.53) | data formatting | bytes 1048576 | tf_op jit(solution)/shard_map/while/body/eval_jaxpr/convert_element_type | solution.py:104
  70.9 1.2 convolution_convert_fusion.3
  72.1 1.6 convert_element_type.145
  73.6 2.2 %copy.53 = bf16[8,32,32,32]{3,2,1,0:T(8,128)(2,1)} copy(bf16[8,32,32,32]{3,1,2,0:T(8,128)(2,1)S(1)} %bitcast.90) | data formatting | bytes 1048576 | tf_op jit(solution)/shard_map/while/body/eval_jaxpr/convert_element_type | solution.py:104
  75.8 3.5 %convert_element_type.146 = bf16[8,32,1024]{2,1,0:T(8,128)(2,1)S(1)} reshape(bf16[8,32,32,32]{3,2,1,0:T(8,128)(2,1)} %copy.53) | data formatting | bytes 1048576 | tf_op jit(solution)/shard_map/while/body/eval_jaxpr/convert_element_type | solution.py:104
  81.6 1.2 convolution_convert_fusion.3
  82.8 1.6 convert_element_type.145
  84.4 2.2 %copy.53 = bf16[8,32,32,32]{3,2,1,0:T(8,128)(2,1)} copy(bf16[8,32,32,32]{3,1,2,0:T(8,128)(2,1)S(1)} %bitcast.90) | data formatting | bytes 1048576 | tf_op jit(solution)/shard_map/while/body/eval_jaxpr/convert_element_type | solution.py:104
  86.6 3.5 %convert_element_type.146 = bf16[8,32,1024]{2,1,0:T(8,128)(2,1)S(1)} reshape(bf16[8,32,32,32]{3,2,1,0:T(8,128)(2,1)} %copy.53) | data formatting | bytes 1048576 | tf_op jit(solution)/shard_map/while/body/eval_jaxpr/convert_element_type | solution.py:104
  90.1 0.9 fusion.73
  91.1 12.2 %all_gather.42 = bf16[32,32]{1,0:T(8,128)(2,1)S(1)} all-gather(bf16[8,32]{1,0:T(8,128)(2,1)S(1)} %get-tuple-element.49), channel_id=1, replica_groups=mesh['groups'=2,'aa'=4,'ba'=4] {'aa'}, dimensions={0}, use_global_device_ids=true | all-gather | bytes 2560 | tf_op jit(solution)/shard_map/all_gather | solution.py:82
  103.3 5.2 %all-gather.1 = bf16[128,32]{1,0:T(8,128)(2,1)S(1)} all-gather(bf16[32,32]{1,0:T(8,128)(2,1)S(1)} %broadcast_select_fusion.2), channel_id=3, replica_groups=mesh['groups'=2,'aa'=4,'ba'=4] {'ba'}, dimensions={0}, use_global_device_ids=true | all-gather | bytes 10240 | tf_op jit(solution)/shard_map/all_gather | solution.py:8
  108.6 1.3 fusion.24
  111.3 7.3 %all_gather.45 = f32[8,32,128]{1,0,2:T(8,128)S(1)} all-gather(f32[8,32,32]{1,0,2:T(8,128)S(1)} %copy.32), channel_id=1, replica_groups=mesh['groups'=2,'aa'=4,'ba'=4] {'ba'}, dimensions={2}, use_global_device_ids=true | all-gather | bytes 163840 | tf_op jit(solution)/shard_map/all_gather | solution.py:124
  118.6 38.3 %all-gather.2 = f32[32,32,128]{1,0,2:T(8,128)S(1)} all-gather(f32[8,32,128]{1,0,2:T(8,128)S(1)} %broadcast_select_fusion), channel_id=4, replica_groups=mesh['groups'=2,'aa'=4,'ba'=4] {'aa'}, dimensions={0}, use_global_device_ids=true | all-gather | bytes 655360 | tf_op jit(solution)/shard_map/all_gather | solution.py:8
  157.4 6.5 %all_gather.37 = bf16[8,128,256]{2,1,0:T(8,128)(2,1)S(1)} all-gather(bf16[8,32,256]{2,1,0:T(8,128)(2,1)S(1)} %fusion.31), channel_id=1, replica_groups=mesh['groups'=2,'aa'=4,'ba'=4] {'ba'}, dimensions={1}, use_global_device_ids=true | all-gather | bytes 655360 | tf_op jit(solution)/shard_map/all_gather | solution.py:139
  166.3 5.4 %all-gather.3 = bf16[4,32,8]{1,2,0:T(8,128)(2,1)S(1)} all-gather(bf16[1,32,8]{1,2,0:T(8,128)(2,1)S(1)} %bitcast.103), channel_id=1, replica_groups=mesh['groups'=2,'aa'=4,'ba'=4] {'ba'}, dimensions={0}, use_global_device_ids=true | all-gather | bytes 2560 | tf_op jit(solution)/shard_map/all_gather | solution.py:140
  172.9 1.1 fusion.4
  (76 shorter events, 18.0 us)
Async XLA Ops:
  0.6 175.3 %copy-start = (bf16[1024,256]{1,0:T(8,128)(2,1)S(1)}, bf16[1024,256]{1,0:T(8,128)(2,1)}, u32[]{:S(2)}) copy-start(bf16[1024,256]{1,0:T(8,128)(2,1)} %param.29) | copy-start | bytes 1572868
  2.8 29.7 %copy-start.7 = (bf16[256,32]{0,1:T(8,128)(2,1)S(1)}, bf16[256,32]{0,1:T(8,128)(2,1)}, u32[]{:S(2)}) copy-start(bf16[256,32]{0,1:T(8,128)(2,1)} %param.20) | copy-start | bytes 49156
  21.1 26.8 %copy-start.1 = (bf16[1024,128]{1,0:T(8,128)(2,1)S(1)}, bf16[1024,128]{1,0:T(8,128)(2,1)}, u32[]{:S(2)}) copy-start(bf16[1024,128]{1,0:T(8,128)(2,1)} %param.21) | copy-start | bytes 786436
  47.9 62.6 %copy-start.11 = (bf16[128,8]{0,1:T(8,128)(2,1)S(1)}, bf16[128,8]{0,1:T(8,128)(2,1)}, u32[]{:S(2)}) copy-start(bf16[128,8]{0,1:T(8,128)(2,1)} %param.22) | copy-start | bytes 6148
  110.0 46.9 %copy-start.3 = (bf16[32,32,128]{2,1,0:T(8,128)(2,1)}, bf16[32,32,128]{2,1,0:T(8,128)(2,1)S(1)}, u32[]{:S(2)}) copy-start(bf16[32,32,128]{2,1,0:T(8,128)(2,1)S(1)} %fusion.24) | copy-start | bytes 786436
  156.9 7.1 %copy-start.4 = (bf16[256,256]{1,0:T(8,128)(2,1)S(1)}, bf16[256,256]{1,0:T(8,128)(2,1)}, u32[]{:S(2)}) copy-start(bf16[256,256]{1,0:T(8,128)(2,1)} %param.25) | copy-start | bytes 393220
  156.9 7.1 %copy-start.5 = (bf16[256,256]{1,0:T(8,128)(2,1)S(1)}, bf16[256,256]{1,0:T(8,128)(2,1)}, u32[]{:S(2)}) copy-start(bf16[256,256]{1,0:T(8,128)(2,1)} %param.24) | copy-start | bytes 393220
  164.9 0.9 copy-start.6
  174.1 1.0 copy-start.9
  174.1 1.0 copy-start.10
  174.1 1.3 copy-start.2
  174.7 1.2 copy-start.8
